TPU v7x, 32 devices: a whole 2x2x4 slice. The times are simulated.
32 devices in a mesh: tile: 8 (over z, x), col: 4 (over y, core).
Axes of the slice: x: 2, y: 2, z: 4, core: 2. Of those that a mesh axis runs over, the one named last changes fastest.
Arguments:
- readings: bfloat16 [64, 4, 512], P(('tile', 'col')), may hold values from -6 to 6
- sensitivity: bfloat16 [32768, 64, 64], P(('tile', 'col')), may hold values from -0.75 to 0.75
- kept_tile: int32 [32768], P(('tile', 'col')), may hold values from 0 to 7
- kept_row: int32 [32768], P(('tile', 'col')), may hold values from 0 to 7
- kept_slab: int32 [32768, 1], P(('tile', 'col')), may hold values from 0 to 31; in each aligned block of 1024 rows (0 to 1023, 1024 to 2047, ...) at most 80 rows name the same one
- kept_block: int32 [32768], P(('tile', 'col')), may hold values from 0 to 8191
Outputs:
- model_update: float32 [4, 256, 65536], P(None, None, ('tile', 'col'))
Inputs may be any that keep to these rules, and one draw needn't show every extreme that they name: `kept_slab`: among the 1024 kept blocks held by one device, at most 80 name one slab, and in every draw some device has exactly 80 blocks naming one slab.
All inputs are finite; a program needn't handle non-finite values.
Results may differ from a plain program's by a relative error of at most 0.0029.
Values may be sent and summed in bfloat16 or wider, within the bound.
A program may use at most 128 MiB of HBM per device.

v0:
```python
import functools

import jax
import jax.numpy as jnp
from jax import lax
from jax.experimental import pallas as pl
from jax.experimental.pallas import tpu as pltpu
from jax.sharding import PartitionSpec as P

NX = 256
NY = 256
NZ = 256
LEVELS = 3
ROOT = 0.7071067811865476
LANES = 128
BUCKET = 8
STEP = 8
AXES = ("tile", "col")


def segments(length):
    coarse = length // 2**LEVELS
    found = [(0, coarse, 2**LEVELS)]
    for level in range(LEVELS):
        found.append((coarse * 2**level, coarse * 2**level, 2 ** (LEVELS - level)))
    return found


def haar_sign(out_index, in_index, length):
    value = jnp.zeros(jnp.broadcast_shapes(out_index.shape, in_index.shape), jnp.float32)
    for number, (start, count, reach) in enumerate(segments(length)):
        inside = (in_index >= start) & (in_index < start + count)
        meets = inside & (out_index // reach == in_index - start)
        sign = jnp.where(out_index % reach < reach // 2, 1.0, -1.0) if number else 1.0
        value = jnp.where(meets, sign, value)
    return value


def haar_scale(in_index, length):
    scale = jnp.zeros(in_index.shape, jnp.float32)
    for start, count, reach in segments(length):
        inside = (in_index >= start) & (in_index < start + count)
        scale = jnp.where(inside, ROOT ** (reach.bit_length() - 1), scale)
    return scale


def y_plan(y_share, width):
    rows = []
    used = {}
    for start, count, reach in segments(NY):
        group = min(start // width, 2)
        for i in range(max(1, y_share // reach)):
            slot = used.get(group, 0)
            used[group] = slot + 1
            rows.append((start, reach, i, slot, group))
    return rows, max(used.values())


def contrib_kernel(ids_ref, table_ref, sens_ref, out_ref):
    rows = ids_ref.shape[0]
    count, width, _ = sens_ref.shape
    vectors = rows // count
    wide = table_ref.shape[1]
    pack = wide // width
    spots = lax.broadcasted_iota(jnp.int32, (rows, table_ref.shape[0]), 1)
    chosen = jnp.where(ids_ref[...] == spots, 1.0, 0.0).astype(jnp.bfloat16)
    picked = jnp.dot(chosen, table_ref[...], preferred_element_type=jnp.float32)
    row = lax.broadcasted_iota(jnp.int32, (rows, wide), 0)
    lane = lax.broadcasted_iota(jnp.int32, (rows, wide), 1)
    own = (row // vectors) % pack == lane // width
    left = jnp.where(own, picked, 0.0).astype(jnp.bfloat16)
    sens = sens_ref[...].reshape(count * width, width)
    step = pack * vectors
    for g in range(count // pack):
        out_ref[g * step : (g + 1) * step, :] = jnp.dot(
            left[g * step : (g + 1) * step, :],
            sens[g * wide : (g + 1) * wide, :],
            preferred_element_type=jnp.float32,
        ).astype(jnp.bfloat16)


def two_part_dot(a, b, split_left):
    whole = a if split_left else b
    high = whole.astype(jnp.bfloat16)
    low = (whole - high.astype(jnp.float32)).astype(jnp.bfloat16)
    if split_left:
        pair = jnp.dot(high, b, preferred_element_type=jnp.float32)
        return pair + jnp.dot(low, b, preferred_element_type=jnp.float32)
    pair = jnp.dot(a, high, preferred_element_type=jnp.float32)
    return pair + jnp.dot(a, low, preferred_element_type=jnp.float32)


def model_kernel(
    plan, vectors, off_ref, vals_ref, ids_ref, hy_ref, hx_ref, hz_ref, scale_ref, out_ref, plane, left, right, total
):
    sources = vals_ref.shape[0]
    slots = vals_ref.shape[1] // vectors
    buckets = NZ // BUCKET
    y_share = hy_ref.shape[0] // (vectors * BUCKET)
    per_y = NY // 64

    def clear(i, carry):
        right[:, pl.ds(pl.multiple_of(i * LANES, LANES), LANES)] = jnp.zeros((NX, LANES), jnp.bfloat16)
        return carry

    lax.fori_loop(0, right.shape[1] // LANES, clear, 0)

    def bucket_step(s, carry):
        layer = lax.broadcasted_iota(jnp.int32, (BUCKET, LANES), 0) + s * BUCKET
        across = lax.broadcasted_iota(jnp.int32, (NX, LANES), 0)

        def chunk(src, block, used):
            base = pl.multiple_of(block * LANES, LANES)
            ids = ids_ref[src, :, pl.ds(base, LANES)]
            vals = vals_ref[src, :, pl.ds(base, LANES)].astype(jnp.float32)
            depth = ids // (NX * per_y)
            x = (ids // per_y) % NX
            b = jnp.minimum(ids % per_y, 2)
            there = depth == layer
            marks = [jnp.where(there & (b == g), 1.0, 0.0) for g in range(3)]
            pieces = []
            for _, _, _, slot, group in plan:
                for v in range(vectors):
                    line = vals[v * slots + slot : v * slots + slot + 1, :]
                    pieces.append(line * marks[group])
            place = pl.ds(pl.multiple_of(used * LANES, LANES), LANES)
            left[:, place] = jnp.concatenate(pieces, axis=0).astype(jnp.bfloat16)
            right[:, place] = jnp.where(x == across, 1.0, 0.0).astype(jnp.bfloat16)
            return used + 1

        def source_step(src, used):
            at = src * (buckets + 1) + s
            low = off_ref[at]
            high = off_ref[at + 1]
            first = low // LANES
            last = jnp.where(high > low, (high + LANES - 1) // LANES, first)
            return lax.fori_loop(first, last, lambda block, n: chunk(src, block, n), used)

        used = lax.fori_loop(0, sources, source_step, 0)
        rounds = (used + STEP - 1) // STEP

        def pad(i, carry):
            left[:, pl.ds(pl.multiple_of(i * LANES, LANES), LANES)] = jnp.zeros((left.shape[0], LANES), jnp.bfloat16)
            return carry

        lax.fori_loop(used, rounds * STEP, pad, 0)
        total[...] = jnp.zeros_like(total)

        def add(i, carry):
            place = pl.ds(pl.multiple_of(i * STEP * LANES, LANES), STEP * LANES)
            total[...] += lax.dot_general(
                left[:, place], right[:, place], (((1,), (1,)), ((), ())), preferred_element_type=jnp.float32
            )
            return carry

        lax.fori_loop(0, rounds, add, 0)
        z = s * BUCKET
        depth_scale = jnp.float32(0.0)
        for start, count, reach in segments(NZ):
            inside = (z >= start) & (z < start + count)
            depth_scale = jnp.where(inside, jnp.float32(ROOT ** (reach.bit_length() - 1)), depth_scale)
        coef = total[...] * (scale_ref[...] * depth_scale)
        along_y = two_part_dot(hy_ref[...], coef, False)
        along_x = two_part_dot(along_y, hx_ref[...], True)
        rows = pl.ds(pl.multiple_of(z, BUCKET), BUCKET)
        for y in range(y_share):
            for v in range(vectors):
                at = (y * vectors + v) * BUCKET
                plane[v, rows, y * NX : (y + 1) * NX] = along_x[at : at + BUCKET, :]
        return carry

    lax.fori_loop(0, buckets, bucket_step, 0)

    def finish(v, carry):
        for y in range(y_share):
            part = plane[v, :, y * NX : (y + 1) * NX]
            out_ref[v, :, y * NX : (y + 1) * NX] = two_part_dot(hz_ref[...], part, False)
        return carry

    lax.fori_loop(0, vectors, finish, 0)


def on_device(readings, sensitivity, kept_tile, kept_row, kept_slab, kept_block):
    devices = lax.axis_size(AXES)
    columns = lax.axis_size("col")
    me = lax.axis_index(AXES)
    kept, width, _ = sensitivity.shape
    vectors = readings.shape[1]
    per_y = NY // width
    layers = NZ // devices
    y_share = NY // devices
    buckets = NZ // BUCKET
    plan, slots = y_plan(y_share, width)

    depth = kept_slab[:, 0] * layers + kept_block // (NX * per_y)
    spot = depth * (NX * per_y) + kept_block % (NX * per_y)
    number = jnp.arange(kept, dtype=jnp.int32)
    key = (depth // BUCKET) * kept + number
    position = jnp.sum((key[None, :] < key[:, None]).astype(jnp.int32), axis=1)
    moved = position[:, None] == number[None, :]
    spots = jnp.sum(jnp.where(moved, spot[:, None], 0), axis=0)
    all_spots = lax.all_to_all(
        jnp.broadcast_to(spots[None], (devices, kept)), AXES, split_axis=0, concat_axis=0, tiled=True
    )
    group = lax.all_to_all(
        jnp.broadcast_to(readings[None], (columns, *readings.shape)), "col", split_axis=0, concat_axis=0, tiled=True
    )
    row_blocks = readings.shape[2] // width
    table = jnp.tile(group.reshape(-1, width), (1, 256 // width))
    ids = (kept_tile[:, None] * vectors + jnp.arange(vectors, dtype=jnp.int32)[None, :]) * row_blocks + kept_row[:, None]
    chunk = 64
    contrib = pl.pallas_call(
        contrib_kernel,
        out_shape=jax.ShapeDtypeStruct((kept * vectors, width), jnp.bfloat16),
        grid=(kept // chunk,),
        in_specs=[
            pl.BlockSpec((chunk * vectors, 1), lambda i: (i, 0)),
            pl.BlockSpec(table.shape, lambda i: (0, 0)),
            pl.BlockSpec((chunk, width, width), lambda i: (i, 0, 0)),
        ],
        out_specs=pl.BlockSpec((chunk * vectors, width), lambda i: (i, 0)),
    )(ids.reshape(kept * vectors, 1), table, sensitivity)
    contrib = contrib.reshape(kept, vectors * width)

    in_y = spot % per_y
    masked = jnp.concatenate([jnp.where((in_y == b)[:, None], contrib, 0) for b in range(per_y)], axis=1)
    row = jnp.arange(per_y * vectors * width, dtype=jnp.int32)[:, None]
    lane = jnp.arange(devices * vectors * slots, dtype=jnp.int32)[None, :]
    y_of_row = row // (vectors * width) * width + row % width
    owner = lane // (vectors * slots)
    spread = jnp.zeros((row.shape[0], lane.shape[1]), jnp.bool_)
    for start, reach, i, slot, _ in plan:
        spread = spread | ((lane % slots == slot) & (y_of_row == start + (owner * y_share) // reach + i))
    spread = spread & (row // width % vectors == lane // slots % vectors)
    sorted_by = jnp.dot(masked, spread.astype(jnp.bfloat16), preferred_element_type=jnp.float32).astype(jnp.bfloat16)
    outgoing = lax.dot_general(
        sorted_by, moved.astype(jnp.bfloat16), (((0,), (0,)), ((), ())), preferred_element_type=jnp.float32
    ).astype(jnp.bfloat16)
    arrived = lax.all_to_all(
        outgoing.reshape(devices, vectors * slots, kept), AXES, split_axis=0, concat_axis=0, tiled=True
    )

    edges = jnp.arange(buckets + 1, dtype=jnp.int32) * (BUCKET * NX * per_y)
    offsets = jnp.sum((all_spots[:, None, :] < edges[None, :, None]).astype(jnp.int32), axis=2).reshape(-1)
    full = jnp.arange(NX, dtype=jnp.int32)
    sign_x = haar_sign(full[None, :], full[:, None], NX).astype(jnp.bfloat16)
    sign_z = haar_sign(full[:, None], full[None, :], NZ).astype(jnp.bfloat16)
    inner = vectors * BUCKET
    needs = jnp.stack([start + (me * y_share) // reach + i for start, reach, i, _, _ in plan]).astype(jnp.int32)
    needs = jnp.repeat(needs, inner)
    line = jnp.arange(y_share * inner, dtype=jnp.int32)
    same = line[:, None] % inner == jnp.arange(len(plan) * inner, dtype=jnp.int32)[None, :] % inner
    sign_y = haar_sign(me * y_share + line[:, None] // inner, needs[None, :], NY)
    sign_y = jnp.where(same, sign_y, 0.0).astype(jnp.bfloat16)
    scale = haar_scale(needs, NY)[:, None] * haar_scale(full, NX)[None, :]
    reach = -(-(2 * devices) // STEP) * STEP * LANES
    vmem = pl.BlockSpec(memory_space=pltpu.VMEM)
    return pl.pallas_call(
        functools.partial(model_kernel, plan, vectors),
        out_shape=jax.ShapeDtypeStruct((vectors, NZ, y_share * NX), jnp.float32),
        in_specs=[pl.BlockSpec(memory_space=pltpu.SMEM)] + [vmem] * 6,
        out_specs=vmem,
        scratch_shapes=[
            pltpu.VMEM((vectors, NZ, y_share * NX), jnp.float32),
            pltpu.VMEM((len(plan) * inner, reach), jnp.bfloat16),
            pltpu.VMEM((NX, reach), jnp.bfloat16),
            pltpu.VMEM((len(plan) * inner, NX), jnp.float32),
        ],
        compiler_params=pltpu.CompilerParams(vmem_limit_bytes=60 * 2**20),
    )(offsets, arrived, all_spots[:, None, :], sign_y, sign_x, sign_z, scale)


def solution(mesh):
    return jax.shard_map(
        on_device,
        mesh=mesh,
        in_specs=(
            P(AXES, None, None),
            P(AXES, None, None),
            P(AXES),
            P(AXES),
            P(AXES, None),
            P(AXES),
        ),
        out_specs=P(None, None, AXES),
        check_vma=False,
    )
```

profile of v0, /device:TPU:0, one launch (start us, length us, event | category | flops | bytes accessed | tf_op | source)
XLA Modules:
  0.0 270.6 jit_solution(999032573663128588)
XLA Ops:
  0.0 1.3 broadcast_in_dim.187
  1.3 4.3 %all-to-all-start.1 = ((bf16[4,2,4,512]{3,2,1,0:T(4,128)(2,1)}), bf16[4,2,4,512]{3,2,1,0:T(4,128)(2,1)S(1)}, u32[]{:S(2)}, u32[]{:S(2)}) async-start(bf16[4,2,4,512]{3,2,1,0:T(4,128)(2,1)} %broadcast_in_dim.187), calls=%async_computation.1 | async-start | bytes 65536 | tf_op jit(solution)/shard_map/all_to_all | solution.py:205
  5.6 0.7 broadcast_multiply_fusion.2
  6.3 0.7 broadcast_compare_fusion.2
  7.0 0.7 fusion.78
  7.9 0.6 convert_reduce_fusion.1
  8.4 0.7 select_reduce_fusion
  9.1 0.7 broadcast_multiply_fusion.1
  9.8 1.0 multiply_add_fusion
  10.9 1.8 add.628.ids_ref
  12.6 23.9 %copy.20.sens_ref = bf16[1024,64,64]{2,1,0:T(8,128)(2,1)} copy(bf16[1024,64,64]{0,2,1:T(8,128)(2,1)} %param.7) | data formatting | bytes 16777216 | tf_op args[1]
  36.6 0.7 broadcast_in_dim.185
  37.3 6.8 %all-to-all-start = ((s32[32,1,1024]{2,1,0:T(1,128)}), s32[32,1,1024]{2,1,0:T(1,128)S(1)}, u32[]{:S(2)}, u32[]{:S(2)}) async-start(s32[32,1,1024]{2,1,0:T(1,128)} %broadcast_in_dim.185), calls=%async_computation | async-start | bytes 262144 | tf_op jit(solution)/shard_map/all_to_all | solution.py:202
  44.1 0.1 tile.10
  44.2 0.1 copy.17
  44.3 0.7 copy.19.table_ref
  45.1 15.9 %shard_map.64 = bf16[4096,64]{1,0:T(8,128)(2,1)} custom-call(s32[4096,1]{1,0:T(8,128)} %add.628.ids_ref, bf16[256,256]{1,0:T(8,128)(2,1)} %copy.19.table_ref, bf16[1024,64,64]{2,1,0:T(8,128)(2,1)} %copy.20.sens_ref), custom_call_target="tpu_custom_call" | custom-call | tf_op jit(solution)/shard_map/pallas_call | solution.py:212
  61.0 1.9 reshape.1182
  62.9 1.0 broadcast_select_fusion.3
  63.9 5.4 %fusion.40 = bf16[512,1024]{1,0:T(8,128)(2,1)} fusion(s32[1024]{0:T(1024)S(1)} %convert_reduce_fusion.1, bf16[1024,256]{1,0:T(8,128)(2,1)S(1)} %get-tuple-element.13, bf16[1024,256]{1,0:T(8,128)(2,1)S(1)} %get-tuple-element.14, bf16[1024,256]{1,0:T(8,128)(2,1)S(1)} %get-tuple-element.15, bf16[1024,256]{1,0:T(8,128)(2,1)S(1)} %get-tuple-element.12, ...), kind=kOutput, calls=%fused_computation.40 | convolution fusion | flops 2171076608 | bytes 3178496 | tf_op jit(solution)/shard_map/dot_general | solution.py:236
  69.3 6.0 %all-to-all-start.2 = ((bf16[32,16,1024]{2,1,0:T(8,128)(2,1)}), bf16[32,16,1024]{2,1,0:T(8,128)(2,1)S(1)}, u32[]{:S(2)}, u32[]{:S(2)}) async-start(bf16[32,16,1024]{2,1,0:T(8,128)(2,1)} %bitcast.2), calls=%async_computation.2 | async-start | bytes 2097152 | tf_op jit(solution)/shard_map/all_to_all | solution.py:239
  75.4 0.1 stack.35
  75.5 0.1 broadcast_in_dim_reshape.3
  75.7 1.0 select_convert_fusion.2.hy_ref
  76.7 0.8 broadcast_multiply_fusion.scale_ref
  77.5 1.3 select_convert_fusion
  78.8 0.7 convert_reduce_fusion
  79.5 0.1 copy.16
  79.6 0.7 reshape.1181.off_ref
  80.3 21.1 %all-to-all-done.2.vals_ref = bf16[32,16,1024]{2,1,0:T(8,128)(2,1)S(1)} async-done(((bf16[32,16,1024]{2,1,0:T(8,128)(2,1)}), bf16[32,16,1024]{2,1,0:T(8,128)(2,1)S(1)}, u32[]{:S(2)}, u32[]{:S(2)}) %all-to-all-start.2) | async-done | bytes 1048608 | tf_op jit(solution)/shard_map/all_to_all | solution.py:239
  101.4 1.0 copy-done
  102.3 168.2 %shard_map.65 = f32[4,256,2048]{2,1,0:T(8,128)} custom-call(s32[1056]{0:T(1024)} %reshape.1181.off_ref, bf16[32,16,1024]{2,1,0:T(8,128)(2,1)} %copy-done, s32[32,1,1024]{2,1,0:T(1,128)} %copy-done.1, bf16[256,256]{1,0:T(8,128)(2,1)} %select_convert_fusion.2.hy_ref, bf16[256,256]{1,0:T(8,128)(2,1)} %get-tuple-element.17.hx_ref, ...), custom_call_target="tpu_custom_call" | custom-call | tf_op jit(solution)/shard_map/pallas_call | solution.py:258
  (32 shorter events, 0.3 us)
Async XLA Ops:
  1.3 35.3 %all-to-all-start.1 = ((bf16[4,2,4,512]{3,2,1,0:T(4,128)(2,1)}), bf16[4,2,4,512]{3,2,1,0:T(4,128)(2,1)S(1)}, u32[]{:S(2)}, u32[]{:S(2)}) async-start(bf16[4,2,4,512]{3,2,1,0:T(4,128)(2,1)} %broadcast_in_dim.187), calls=%async_computation.1 | async-start | bytes 65536 | tf_op jit(solution)/shard_map/all_to_all | solution.py:205
  37.3 32.0 %all-to-all-start = ((s32[32,1,1024]{2,1,0:T(1,128)}), s32[32,1,1024]{2,1,0:T(1,128)S(1)}, u32[]{:S(2)}, u32[]{:S(2)}) async-start(s32[32,1,1024]{2,1,0:T(1,128)} %broadcast_in_dim.185), calls=%async_computation | async-start | bytes 262144 | tf_op jit(solution)/shard_map/all_to_all | solution.py:202
  69.3 32.1 %copy-start.1 = (s32[32,1,1024]{2,1,0:T(1,128)}, s32[32,1,1024]{2,1,0:T(1,128)S(1)}, u32[]{:S(2)}) copy-start(s32[32,1,1024]{2,1,0:T(1,128)S(1)} %all-to-all-done.ids_ref) | copy-start | bytes 393220
  69.3 32.0 %all-to-all-start.2 = ((bf16[32,16,1024]{2,1,0:T(8,128)(2,1)}), bf16[32,16,1024]{2,1,0:T(8,128)(2,1)S(1)}, u32[]{:S(2)}, u32[]{:S(2)}) async-start(bf16[32,16,1024]{2,1,0:T(8,128)(2,1)} %bitcast.2), calls=%async_computation.2 | async-start | bytes 2097152 | tf_op jit(solution)/shard_map/all_to_all | solution.py:239
  101.4 1.0 copy-start
where the time goes:
time: 272 us; the launch traced here: 271 us
  Pallas kernels  184 us (68%)
  local copies, waits for them, and re-layouts  32.7 us (12%)
  waiting for transfers between devices  21.1 us (8%)
  starting transfers between devices  17.1 us (6%)
  other arithmetic  9.97 us (4%)
  matrix products  5.42 us (2%)
    pallas_call x1, Pallas kernels, on_device(): pl.pallas_call(functools.partial(model_kernel, plan, vectors), out_shape=...  168 us
    unnamed x6, local copies, waits for them, and re-layouts  25 us
    all_to_all x1, waiting for transfers between devices, on_device(): lax.all_to_all(outgoing.reshape(devices, vectors * slots, kept), AXES, sp...  21.1 us
    pallas_call x1, Pallas kernels, on_device(): pl.pallas_call(contrib_kernel, out_shape=jax.ShapeDtypeStruct((kept * vec...  15.9 us
    all_to_all x1, starting transfers between devices, on_device(): lax.all_to_all(jnp.broadcast_to(spots[None], (devices, kept)), AXES, spli...  6.8 us
    all_to_all x1, starting transfers between devices, on_device(): lax.all_to_all(outgoing.reshape(devices, vectors * slots, kept), AXES, sp...  6.01 us
  transfers between devices with their start and end apart: 3, of which 1 were waited for; matrix products, arithmetic and copies ran while one was open for 17% of the time, Pallas kernels for 6%

commit v1 on v0

v1 whole, which is shorter than its diff:
```python
import functools

import jax
import jax.numpy as jnp
from jax import lax
from jax.experimental import pallas as pl
from jax.experimental.pallas import tpu as pltpu
from jax.sharding import PartitionSpec as P

NX = 256
NY = 256
NZ = 256
LEVELS = 3
ROOT = 0.7071067811865476
LANES = 128
BUCKET = 8
MOVES = 8
ROUND = 512
AXES = ("tile", "col")


def segments(length):
    coarse = length // 2**LEVELS
    found = [(0, coarse, 2**LEVELS)]
    for level in range(LEVELS):
        found.append((coarse * 2**level, coarse * 2**level, 2 ** (LEVELS - level)))
    return found


def haar_sign(out_index, in_index, length):
    value = jnp.zeros(jnp.broadcast_shapes(out_index.shape, in_index.shape), jnp.float32)
    for number, (start, count, reach) in enumerate(segments(length)):
        inside = (in_index >= start) & (in_index < start + count)
        meets = inside & (out_index // reach == in_index - start)
        sign = jnp.where(out_index % reach < reach // 2, 1.0, -1.0) if number else 1.0
        value = jnp.where(meets, sign, value)
    return value


def haar_scale(in_index, length):
    scale = jnp.zeros(in_index.shape, jnp.float32)
    for start, count, reach in segments(length):
        inside = (in_index >= start) & (in_index < start + count)
        scale = jnp.where(inside, ROOT ** (reach.bit_length() - 1), scale)
    return scale


def y_plan(y_share, width):
    rows = []
    used = {}
    for start, count, reach in segments(NY):
        group = min(start // width, 2)
        for i in range(max(1, y_share // reach)):
            slot = used.get(group, 0)
            used[group] = slot + 1
            rows.append((start, reach, i, slot, group))
    return rows, max(used.values())


def contrib_kernel(ids_ref, table_ref, sens_ref, out_ref):
    width, columns, lanes = sens_ref.shape
    vectors = table_ref.shape[0] // width
    spots = lax.broadcasted_iota(jnp.int32, (table_ref.shape[1], lanes), 0)
    chosen = jnp.where(ids_ref[...] == spots, 1.0, 0.0).astype(jnp.bfloat16)
    picked = jnp.dot(table_ref[...], chosen, preferred_element_type=jnp.float32)
    sums = [jnp.zeros((columns, lanes), jnp.float32) for _ in range(vectors)]
    for r in range(width):
        sens = sens_ref[r].astype(jnp.float32)
        for v in range(vectors):
            sums[v] = sums[v] + sens * picked[v * width + r : v * width + r + 1, :]
    for v in range(vectors):
        out_ref[v * columns : (v + 1) * columns, :] = sums[v].astype(jnp.bfloat16)


def two_part_dot(a, b, split_left):
    whole = a if split_left else b
    high = whole.astype(jnp.bfloat16)
    low = (whole - high.astype(jnp.float32)).astype(jnp.bfloat16)
    if split_left:
        pair = jnp.dot(high, b, preferred_element_type=jnp.float32)
        return pair + jnp.dot(low, b, preferred_element_type=jnp.float32)
    pair = jnp.dot(a, high, preferred_element_type=jnp.float32)
    return pair + jnp.dot(a, low, preferred_element_type=jnp.float32)


def model_kernel(
    plan, vectors, off_ref, to_ref, start_ref, vals_ref, ids_ref, hy_ref, hx_ref, hz_ref, scale_ref, out_ref,
    plane, vals_in, ids_in, left, right, total
):
    sources = vals_ref.shape[0]
    kept = vals_ref.shape[2]
    slots = vals_ref.shape[1] // vectors
    buckets = NZ // BUCKET
    y_share = hy_ref.shape[0] // (vectors * BUCKET)
    per_y = NY // 64
    y_bits = per_y.bit_length() - 1
    x_bits = NX.bit_length() - 1
    window = 2 * LANES

    def clear(i, carry):
        place = pl.ds(pl.multiple_of(i * window, LANES), window)
        ids_in[:, place] = jnp.full((BUCKET, window), -1, jnp.int32)
        vals_in[:, place] = jnp.zeros((vals_in.shape[0], window), jnp.float32)
        return carry

    lax.fori_loop(0, ids_in.shape[1] // window, clear, 0)
    lane = lax.broadcasted_iota(jnp.int32, (BUCKET, window), 1)
    lanes_all = lax.broadcasted_iota(jnp.int32, (vals_in.shape[0], window), 1)

    def move(step, carry):
        s = step // (sources // MOVES)
        for u in range(MOVES):
            src = (step % (sources // MOVES)) * MOVES + u
            low = off_ref[src * (buckets + 1) + s]
            high = off_ref[src * (buckets + 1) + s + 1]
            to = to_ref[src * buckets + s]
            base = jnp.minimum((low // LANES) * LANES, kept - window)
            begin = to % LANES
            shift = (begin - (low - base) + 2 * window) % window
            place = pl.ds(pl.multiple_of(base, LANES), window)
            target = pl.ds(pl.multiple_of((to // LANES) * LANES, LANES), window)
            ids = jnp.broadcast_to(ids_ref[src, :, place], (BUCKET, window))
            vals = vals_ref[src, :, place].astype(jnp.float32)
            ids = pltpu.roll(ids, shift, 1)
            vals = pltpu.roll(vals, shift, 1)
            end = begin + high - low
            ids_in[:, target] = jnp.where((lane >= begin) & (lane < end), ids, ids_in[:, target])
            vals_in[:, target] = jnp.where((lanes_all >= begin) & (lanes_all < end), vals, vals_in[:, target])
        return carry

    lax.fori_loop(0, buckets * (sources // MOVES), move, 0)

    def bucket_step(s, carry):
        layer = lax.broadcasted_iota(jnp.int32, (BUCKET, ROUND), 0) + s * BUCKET
        row = lax.broadcasted_iota(jnp.int32, (BUCKET, ROUND), 0)
        first = start_ref[s]
        total[...] = jnp.zeros_like(total)

        def add(i, carry):
            place = pl.ds(pl.multiple_of(first + i * ROUND, LANES), ROUND)
            ids = ids_in[:, place]
            vals = vals_in[:, place]
            x = (ids >> y_bits) & (NX - 1)
            b = jnp.minimum(ids & (per_y - 1), 2)
            there = (ids >> (y_bits + x_bits)) == layer
            marks = [jnp.where(there & (b == g), 1.0, 0.0) for g in range(3)]
            pieces = []
            for _, _, _, slot, group in plan:
                for v in range(vectors):
                    line = vals[v * slots + slot : v * slots + slot + 1, :]
                    pieces.append(line * marks[group])
            left[...] = jnp.concatenate(pieces, axis=0).astype(jnp.bfloat16)
            hits = [jnp.where(x - row == n, 1.0, 0.0) for n in range(0, NX, BUCKET)]
            right[...] = jnp.concatenate(hits, axis=0).astype(jnp.bfloat16)
            total[...] += lax.dot_general(
                left[...], right[...], (((1,), (1,)), ((), ())), preferred_element_type=jnp.float32
            )
            return carry

        lax.fori_loop(0, (start_ref[s + 1] - first) // ROUND, add, 0)
        z = s * BUCKET
        depth_scale = jnp.float32(0.0)
        for start, count, reach in segments(NZ):
            inside = (z >= start) & (z < start + count)
            depth_scale = jnp.where(inside, jnp.float32(ROOT ** (reach.bit_length() - 1)), depth_scale)
        coef = total[...] * (scale_ref[...] * depth_scale)
        along_y = two_part_dot(hy_ref[...], coef, False)
        along_x = two_part_dot(along_y, hx_ref[...], True)
        rows = pl.ds(pl.multiple_of(z, BUCKET), BUCKET)
        for y in range(y_share):
            for v in range(vectors):
                at = (y * vectors + v) * BUCKET
                plane[v, rows, y * NX : (y + 1) * NX] = along_x[at : at + BUCKET, :]
        return carry

    lax.fori_loop(0, buckets, bucket_step, 0)

    def finish(v, carry):
        for y in range(y_share):
            part = plane[v, :, y * NX : (y + 1) * NX]
            out_ref[v, :, y * NX : (y + 1) * NX] = two_part_dot(hz_ref[...], part, False)
        return carry

    lax.fori_loop(0, vectors, finish, 0)


def on_device(readings, sensitivity, kept_tile, kept_row, kept_slab, kept_block):
    devices = lax.axis_size(AXES)
    columns = lax.axis_size("col")
    me = lax.axis_index(AXES)
    kept, width, _ = sensitivity.shape
    vectors = readings.shape[1]
    per_y = NY // width
    layers = NZ // devices
    y_share = NY // devices
    buckets = NZ // BUCKET
    plan, slots = y_plan(y_share, width)

    depth = kept_slab[:, 0] * layers + kept_block // (NX * per_y)
    spot = depth * (NX * per_y) + kept_block % (NX * per_y)
    number = jnp.arange(kept, dtype=jnp.int32)
    key = (depth // BUCKET) * kept + number
    position = jnp.sum((key[None, :] < key[:, None]).astype(jnp.int32), axis=1)
    moved = position[:, None] == number[None, :]
    spots = jnp.sum(jnp.where(moved, spot[:, None], 0), axis=0)
    all_spots = lax.all_to_all(
        jnp.broadcast_to(spots[None], (devices, kept)), AXES, split_axis=0, concat_axis=0, tiled=True
    )
    group = lax.all_to_all(
        jnp.broadcast_to(readings[None], (columns, *readings.shape)), "col", split_axis=0, concat_axis=0, tiled=True
    )
    row_blocks = readings.shape[2] // width
    table = group.reshape(-1, vectors, row_blocks, width).transpose(1, 3, 0, 2).reshape(vectors * width, -1)
    ids = (kept_tile * row_blocks + kept_row)[None, :]
    contrib = pl.pallas_call(
        contrib_kernel,
        out_shape=jax.ShapeDtypeStruct((vectors * width, kept), jnp.bfloat16),
        grid=(kept // LANES,),
        in_specs=[
            pl.BlockSpec((1, LANES), lambda i: (0, i)),
            pl.BlockSpec(table.shape, lambda i: (0, 0)),
            pl.BlockSpec((width, width, LANES), lambda i: (0, 0, i)),
        ],
        out_specs=pl.BlockSpec((vectors * width, LANES), lambda i: (0, i)),
    )(ids, table, sensitivity.transpose(1, 2, 0))

    in_y = spot % per_y
    masked = jnp.concatenate([jnp.where((in_y == b)[None, :], contrib, 0) for b in range(per_y)], axis=0)
    row = jnp.arange(per_y * vectors * width, dtype=jnp.int32)[None, :]
    lane = jnp.arange(devices * vectors * slots, dtype=jnp.int32)[:, None]
    y_of_row = row // (vectors * width) * width + row % width
    owner = lane // (vectors * slots)
    spread = jnp.zeros((lane.shape[0], row.shape[1]), jnp.bool_)
    for start, reach, i, slot, _ in plan:
        spread = spread | ((lane % slots == slot) & (y_of_row == start + (owner * y_share) // reach + i))
    spread = spread & (row // width % vectors == lane // slots % vectors)
    chosen = jnp.dot(spread.astype(jnp.bfloat16), masked, preferred_element_type=jnp.float32).astype(jnp.bfloat16)
    outgoing = jnp.dot(chosen, moved.astype(jnp.bfloat16), preferred_element_type=jnp.float32).astype(jnp.bfloat16)
    arrived = lax.all_to_all(
        outgoing.reshape(devices, vectors * slots, kept), AXES, split_axis=0, concat_axis=0, tiled=True
    )

    edges = jnp.arange(buckets + 1, dtype=jnp.int32) * (BUCKET * NX * per_y)
    offsets = jnp.sum((all_spots[:, None, :] < edges[None, :, None]).astype(jnp.int32), axis=2)
    counts = offsets[:, 1:] - offsets[:, :-1]
    source = jnp.arange(devices, dtype=jnp.int32)
    ahead = jnp.sum(jnp.where(source[:, None, None] > source[None, :, None], counts[None], 0), axis=1)
    rounds = (jnp.sum(counts, axis=0) + ROUND - 1) // ROUND
    bucket = jnp.arange(buckets + 1, dtype=jnp.int32)
    starts = jnp.sum(jnp.where(bucket[:, None] > bucket[None, :-1], rounds[None, :], 0), axis=1) * ROUND
    to = ahead + starts[None, :-1]
    full = jnp.arange(NX, dtype=jnp.int32)
    sign_x = haar_sign(full[None, :], full[:, None], NX).astype(jnp.bfloat16)
    sign_z = haar_sign(full[:, None], full[None, :], NZ).astype(jnp.bfloat16)
    inner = vectors * BUCKET
    needs = jnp.stack([start + (me * y_share) // reach + i for start, reach, i, _, _ in plan]).astype(jnp.int32)
    needs = jnp.repeat(needs, inner)
    line = jnp.arange(y_share * inner, dtype=jnp.int32)
    same = line[:, None] % inner == jnp.arange(len(plan) * inner, dtype=jnp.int32)[None, :] % inner
    sign_y = haar_sign(me * y_share + line[:, None] // inner, needs[None, :], NY)
    sign_y = jnp.where(same, sign_y, 0.0).astype(jnp.bfloat16)
    scale = haar_scale(needs, NY)[:, None] * haar_scale(full, NX)[None, :]
    room = devices * kept + buckets * ROUND + 2 * LANES
    vmem = pl.BlockSpec(memory_space=pltpu.VMEM)
    smem = pl.BlockSpec(memory_space=pltpu.SMEM)
    return pl.pallas_call(
        functools.partial(model_kernel, plan, vectors),
        out_shape=jax.ShapeDtypeStruct((vectors, NZ, y_share * NX), jnp.float32),
        in_specs=[smem] * 3 + [vmem] * 6,
        out_specs=vmem,
        scratch_shapes=[
            pltpu.VMEM((vectors, NZ, y_share * NX), jnp.float32),
            pltpu.VMEM((vectors * slots, room), jnp.float32),
            pltpu.VMEM((BUCKET, room), jnp.int32),
            pltpu.VMEM((len(plan) * inner, ROUND), jnp.bfloat16),
            pltpu.VMEM((NX, ROUND), jnp.bfloat16),
            pltpu.VMEM((len(plan) * inner, NX), jnp.float32),
        ],
        compiler_params=pltpu.CompilerParams(vmem_limit_bytes=60 * 2**20),
    )(offsets.reshape(-1), to.reshape(-1), starts, arrived, all_spots[:, None, :], sign_y, sign_x, sign_z, scale)


def solution(mesh):
    return jax.shard_map(
        on_device,
        mesh=mesh,
        in_specs=(
            P(AXES, None, None),
            P(AXES, None, None),
            P(AXES),
            P(AXES),
            P(AXES, None),
            P(AXES),
        ),
        out_specs=P(None, None, AXES),
        check_vma=False,
    )
```

time: 272 us -> 144 us (0.53)
  Pallas kernels: 184 us -> 83.9 us
  local copies, waits for them, and re-layouts: 32.7 us -> 5.78 us
    pallas_call x1, Pallas kernels: 168 us -> 74.1 us  [on_device(): pl.pallas_call(functools.partial(model_kernel, plan, vectors), out_shape=...]
    unnamed x6 -> x7, local copies, waits for them, and re-layouts: 25 us -> 1.01 us
    pallas_call x1, Pallas kernels: 15.9 us -> 9.77 us  [on_device(): pl.pallas_call(contrib_kernel, out_shape=jax.ShapeDtypeStruct((vectors *...]
  transfers between devices with their start and end apart: 3 -> 3, of which waited for: 1 -> 1; matrix products, arithmetic and copies ran while one was open for 17% -> 13% of each run, Pallas kernels for 6% -> 7%
where the time goes in v1:
time: 144 us
  Pallas kernels  83.9 us (58%)
  waiting for transfers between devices  20.3 us (14%)
  starting transfers between devices  16.9 us (12%)
  other arithmetic  10.9 us (8%)
  local copies, waits for them, and re-layouts  5.78 us (4%)
  matrix products  5.44 us (4%)
    pallas_call x1, Pallas kernels, on_device(): pl.pallas_call(functools.partial(model_kernel, plan, vectors), out_shape=...  74.1 us
    all_to_all x1, waiting for transfers between devices, on_device(): lax.all_to_all(outgoing.reshape(devices, vectors * slots, kept), AXES, sp...  20.3 us
    pallas_call x1, Pallas kernels, on_device(): pl.pallas_call(contrib_kernel, out_shape=jax.ShapeDtypeStruct((vectors *...  9.77 us
    all_to_all x1, starting transfers between devices, on_device(): lax.all_to_all(jnp.broadcast_to(spots[None], (devices, kept)), AXES, spli...  6.8 us
    all_to_all x1, starting transfers between devices, on_device(): lax.all_to_all(outgoing.reshape(devices, vectors * slots, kept), AXES, sp...  5.83 us
    dot_general x1, matrix products, on_device(): jnp.dot(chosen, moved.astype(jnp.bfloat16), preferred_element_type=jnp.fl...  5.44 us
    all_to_all x1, starting transfers between devices, on_device(): lax.all_to_all(jnp.broadcast_to(readings[None], (columns, *readings.shape...  4.26 us
  transfers between devices with their start and end apart: 3, of which 1 were waited for; matrix products, arithmetic and copies ran while one was open for 13% of the time, Pallas kernels for 7%

profile of v1, /device:TPU:0, one launch (start us, length us, event | category | flops | bytes accessed | tf_op | source)
XLA Modules:
  0.0 143.5 jit_solution(14568480261447604133)
XLA Ops:
  0.0 1.3 broadcast_in_dim.232
  1.3 4.3 %all-to-all-start.1 = ((bf16[4,2,4,512]{3,2,1,0:T(4,128)(2,1)}), bf16[4,2,4,512]{3,2,1,0:T(4,128)(2,1)S(1)}, u32[]{:S(2)}, u32[]{:S(2)}) async-start(bf16[4,2,4,512]{3,2,1,0:T(4,128)(2,1)} %broadcast_in_dim.232), calls=%async_computation.1 | async-start | bytes 65536 | tf_op jit(solution)/shard_map/all_to_all | solution.py:209
  5.8 0.1 stack.35
  6.1 0.7 broadcast_multiply_fusion.1
  6.8 0.7 fusion.71
  7.5 0.7 broadcast_compare_fusion.2
  8.3 0.6 convert_reduce_fusion.1
  8.9 0.7 select_reduce_fusion
  9.5 0.7 iota_compare_fusion.12
  10.2 1.3 multiply_add_fusion
  11.5 0.7 broadcast_in_dim.224
  12.2 6.8 %all-to-all-start = ((s32[32,1,1024]{2,1,0:T(1,128)}), s32[32,1,1024]{2,1,0:T(1,128)S(1)}, u32[]{:S(2)}, u32[]{:S(2)}) async-start(s32[32,1,1024]{2,1,0:T(1,128)} %broadcast_in_dim.224), calls=%async_computation | async-start | bytes 262144 | tf_op jit(solution)/shard_map/all_to_all | solution.py:206
  19.0 0.1 reshape.1177
  19.2 0.1 reshape.1178
  19.3 0.7 copy.17.table_ref
  20.0 9.8 %shard_map.64 = bf16[256,1024]{1,0:T(8,128)(2,1)} custom-call(s32[1,1024]{1,0:T(1,128)} %bitcast.26, bf16[256,64]{1,0:T(8,128)(2,1)} %copy.17.table_ref, bf16[64,64,1024]{2,1,0:T(8,128)(2,1)} %bitcast.21), custom_call_target="tpu_custom_call" | custom-call | tf_op jit(solution)/shard_map/pallas_call | solution.py:215
  29.8 1.2 broadcast_select_fusion.3
  31.0 5.4 %fusion.40 = bf16[512,1024]{1,0:T(8,128)(2,1)} fusion(bf16[256,1024]{1,0:T(8,128)(2,1)S(1)} %get-tuple-element.15, bf16[256,1024]{1,0:T(8,128)(2,1)S(1)} %get-tuple-element.16, bf16[256,1024]{1,0:T(8,128)(2,1)S(1)} %get-tuple-element.17, bf16[256,1024]{1,0:T(8,128)(2,1)S(1)} %get-tuple-element.14, s32[1024]{0:T(1024)S(1)} %get-tuple-element.26, ...), kind=kOutput, calls=%fused_computation.40 | convolution fusion | flops 2170028032 | bytes 4222976 | tf_op jit(solution)/shard_map/dot_general | solution.py:238
  36.4 5.8 %all-to-all-start.2 = ((bf16[32,16,1024]{2,1,0:T(8,128)(2,1)}), bf16[32,16,1024]{2,1,0:T(8,128)(2,1)S(1)}, u32[]{:S(2)}, u32[]{:S(2)}) async-start(bf16[32,16,1024]{2,1,0:T(8,128)(2,1)} %bitcast.4), calls=%async_computation.2 | async-start | bytes 2097152 | tf_op jit(solution)/shard_map/all_to_all | solution.py:239
  42.3 1.0 select_convert_fusion.2.hy_ref
  43.2 0.8 broadcast_multiply_fusion.scale_ref
  44.1 1.3 select_convert_fusion
  45.4 0.7 convert_reduce_fusion
  46.1 0.1 copy.13
  46.2 0.7 reshape.1176.off_ref
  46.9 0.1 fusion.107
  47.1 0.1 select_reduce_fusion.2
  47.2 0.2 select_reduce_fusion.1
  47.5 0.7 add.580.to_ref
  48.1 20.3 %all-to-all-done.2.vals_ref = bf16[32,16,1024]{2,1,0:T(8,128)(2,1)S(1)} async-done(((bf16[32,16,1024]{2,1,0:T(8,128)(2,1)}), bf16[32,16,1024]{2,1,0:T(8,128)(2,1)S(1)}, u32[]{:S(2)}, u32[]{:S(2)}) %all-to-all-start.2) | async-done | bytes 1048608 | tf_op jit(solution)/shard_map/all_to_all | solution.py:239
  68.5 1.0 copy-done
  69.4 74.1 %shard_map.65 = f32[4,256,2048]{2,1,0:T(8,128)} custom-call(s32[1056]{0:T(1024)} %reshape.1176.off_ref, s32[1024]{0:T(1024)} %add.580.to_ref, s32[33]{0:T(128)} %copy-done.2, bf16[32,16,1024]{2,1,0:T(8,128)(2,1)} %copy-done, s32[32,1,1024]{2,1,0:T(1,128)} %copy-done.1, bf16[256,256]{1,0:T(8,128)(2,1)} %select_convert_fusion.2.hy_ref, ...), custom_call_target="tpu_custom_call" | custom-call | tf_op jit(solution)/shard_map/pallas_call | solution.py:266
  (41 shorter events, 0.5 us)
Async XLA Ops:
  1.3 10.2 %all-to-all-start.1 = ((bf16[4,2,4,512]{3,2,1,0:T(4,128)(2,1)}), bf16[4,2,4,512]{3,2,1,0:T(4,128)(2,1)S(1)}, u32[]{:S(2)}, u32[]{:S(2)}) async-start(bf16[4,2,4,512]{3,2,1,0:T(4,128)(2,1)} %broadcast_in_dim.232), calls=%async_computation.1 | async-start | bytes 65536 | tf_op jit(solution)/shard_map/all_to_all | solution.py:209
  12.2 24.2 %all-to-all-start = ((s32[32,1,1024]{2,1,0:T(1,128)}), s32[32,1,1024]{2,1,0:T(1,128)S(1)}, u32[]{:S(2)}, u32[]{:S(2)}) async-start(s32[32,1,1024]{2,1,0:T(1,128)} %broadcast_in_dim.224), calls=%async_computation | async-start | bytes 262144 | tf_op jit(solution)/shard_map/all_to_all | solution.py:206
  36.4 32.1 %copy-start.1 = (s32[32,1,1024]{2,1,0:T(1,128)}, s32[32,1,1024]{2,1,0:T(1,128)S(1)}, u32[]{:S(2)}) copy-start(s32[32,1,1024]{2,1,0:T(1,128)S(1)} %all-to-all-done.ids_ref) | copy-start | bytes 393220
  36.4 32.0 %all-to-all-start.2 = ((bf16[32,16,1024]{2,1,0:T(8,128)(2,1)}), bf16[32,16,1024]{2,1,0:T(8,128)(2,1)S(1)}, u32[]{:S(2)}, u32[]{:S(2)}) async-start(bf16[32,16,1024]{2,1,0:T(8,128)(2,1)} %bitcast.4), calls=%async_computation.2 | async-start | bytes 2097152 | tf_op jit(solution)/shard_map/all_to_all | solution.py:239
  47.4 21.0 %copy-start.2 = (s32[33]{0:T(128)}, s32[33]{0:T(128)S(1)}, u32[]{:S(2)}) copy-start(s32[33]{0:T(128)S(1)} %broadcast_multiply_fusion.2.start_ref) | copy-start | bytes 400
  68.5 1.0 copy-start

commit v2 on v1

--- a/solution.py
+++ b/solution.py
@@ -14,7 +14,7 @@
 ROOT = 0.7071067811865476
 LANES = 128
 BUCKET = 8
-MOVES = 8
+MOVES = 16
 ROUND = 512
 AXES = ("tile", "col")
 
@@ -177,8 +177,8 @@
 
     def finish(v, carry):
         for y in range(y_share):
-            part = plane[v, :, y * NX : (y + 1) * NX]
-            out_ref[v, :, y * NX : (y + 1) * NX] = two_part_dot(hz_ref[...], part, False)
+            part = plane[v, :, y * NX : (y + 1) * NX].astype(jnp.bfloat16)
+            out_ref[v, :, y * NX : (y + 1) * NX] = jnp.dot(hz_ref[...], part, preferred_element_type=jnp.float32)
         return carry
 
     lax.fori_loop(0, vectors, finish, 0)
@@ -224,7 +224,8 @@
         out_specs=pl.BlockSpec((vectors * width, LANES), lambda i: (0, i)),
     )(ids, table, sensitivity.transpose(1, 2, 0))
 
-    in_y = spot % per_y
+    contrib = jnp.dot(contrib, moved.astype(jnp.bfloat16), preferred_element_type=jnp.float32).astype(jnp.bfloat16)
+    in_y = spots % per_y
     masked = jnp.concatenate([jnp.where((in_y == b)[None, :], contrib, 0) for b in range(per_y)], axis=0)
     row = jnp.arange(per_y * vectors * width, dtype=jnp.int32)[None, :]
     lane = jnp.arange(devices * vectors * slots, dtype=jnp.int32)[:, None]
@@ -234,8 +235,7 @@
     for start, reach, i, slot, _ in plan:
         spread = spread | ((lane % slots == slot) & (y_of_row == start + (owner * y_share) // reach + i))
     spread = spread & (row // width % vectors == lane // slots % vectors)
-    chosen = jnp.dot(spread.astype(jnp.bfloat16), masked, preferred_element_type=jnp.float32).astype(jnp.bfloat16)
-    outgoing = jnp.dot(chosen, moved.astype(jnp.bfloat16), preferred_element_type=jnp.float32).astype(jnp.bfloat16)
+    outgoing = jnp.dot(spread.astype(jnp.bfloat16), masked, preferred_element_type=jnp.float32).astype(jnp.bfloat16)
     arrived = lax.all_to_all(
         outgoing.reshape(devices, vectors * slots, kept), AXES, split_axis=0, concat_axis=0, tiled=True
     )

time: 144 us -> 141 us (0.979)
  other arithmetic: 10.9 us -> 8.4 us
  Pallas kernels: 83.9 us -> 81.6 us
    pallas_call x1, Pallas kernels: 74.1 us -> 71.9 us  [on_device(): pl.pallas_call(functools.partial(model_kernel, plan, vectors), out_shape=...]
    dot_general x1 -> x2, matrix products: 5.44 us -> 6.55 us  [the longest x1 4.37 us: on_device(): jnp.dot(spread.astype(jnp.bfloat16), masked, preferred_element_type=jnp.f...]
where the time goes in v2:
time: 141 us; the launch traced here: 140 us
  Pallas kernels  81.6 us (58%)
  waiting for transfers between devices  20.3 us (14%)
  starting transfers between devices  16.9 us (12%)
  other arithmetic  8.4 us (6%)
  matrix products  6.55 us (5%)
  local copies, waits for them, and re-layouts  5.78 us (4%)
    pallas_call x1, Pallas kernels, on_device(): pl.pallas_call(functools.partial(model_kernel, plan, vectors), out_shape=...  71.9 us
    all_to_all x1, waiting for transfers between devices, on_device(): lax.all_to_all(outgoing.reshape(devices, vectors * slots, kept), AXES, sp...  20.3 us
    pallas_call x1, Pallas kernels, on_device(): pl.pallas_call(contrib_kernel, out_shape=jax.ShapeDtypeStruct((vectors *...  9.77 us
    all_to_all x1, starting transfers between devices, on_device(): lax.all_to_all(jnp.broadcast_to(spots[None], (devices, kept)), AXES, spli...  6.8 us
    all_to_all x1, starting transfers between devices, on_device(): lax.all_to_all(outgoing.reshape(devices, vectors * slots, kept), AXES, sp...  5.83 us
    dot_general x1, matrix products, on_device(): jnp.dot(spread.astype(jnp.bfloat16), masked, preferred_element_type=jnp.f...  4.37 us
    all_to_all x1, starting transfers between devices, on_device(): lax.all_to_all(jnp.broadcast_to(readings[None], (columns, *readings.shape...  4.26 us
  transfers between devices with their start and end apart: 3, of which 1 were waited for; matrix products, arithmetic and copies ran while one was open for 13% of the time, Pallas kernels for 7%

profile of v2, /device:TPU:0, one launch (start us, length us, event | category | flops | bytes accessed | tf_op | source)
XLA Modules:
  0.0 139.9 jit_solution(9776757247498948059)
XLA Ops:
  0.0 1.3 broadcast_in_dim.232
  1.3 4.3 %all-to-all-start.1 = ((bf16[4,2,4,512]{3,2,1,0:T(4,128)(2,1)}), bf16[4,2,4,512]{3,2,1,0:T(4,128)(2,1)S(1)}, u32[]{:S(2)}, u32[]{:S(2)}) async-start(bf16[4,2,4,512]{3,2,1,0:T(4,128)(2,1)} %broadcast_in_dim.232), calls=%async_computation.1 | async-start | bytes 65536 | tf_op jit(solution)/shard_map/all_to_all | solution.py:209
  5.8 0.1 stack.35
  5.9 0.1 broadcast_in_dim.237
  6.0 0.1 broadcast_in_dim_reshape.3
  6.2 0.7 broadcast_multiply_fusion.1
  6.9 0.7 fusion.67
  7.6 0.6 convert_reduce_fusion.1
  8.1 0.7 select_reduce_fusion
  8.8 1.3 multiply_add_fusion
  10.1 0.7 broadcast_in_dim.224
  10.8 6.8 %all-to-all-start = ((s32[32,1,1024]{2,1,0:T(1,128)}), s32[32,1,1024]{2,1,0:T(1,128)S(1)}, u32[]{:S(2)}, u32[]{:S(2)}) async-start(s32[32,1,1024]{2,1,0:T(1,128)} %broadcast_in_dim.224), calls=%async_computation | async-start | bytes 262144 | tf_op jit(solution)/shard_map/all_to_all | solution.py:206
  17.7 0.1 reshape.1196
  17.8 0.1 reshape.1197
  17.9 0.7 copy.17.table_ref
  18.6 9.8 %shard_map.64 = bf16[256,1024]{1,0:T(8,128)(2,1)} custom-call(s32[1,1024]{1,0:T(1,128)} %bitcast.24, bf16[256,64]{1,0:T(8,128)(2,1)} %copy.17.table_ref, bf16[64,64,1024]{2,1,0:T(8,128)(2,1)} %bitcast.21), custom_call_target="tpu_custom_call" | custom-call | tf_op jit(solution)/shard_map/pallas_call | solution.py:215
  28.4 2.2 %broadcast_select_fusion.3 = (bf16[256,1024]{1,0:T(8,128)(2,1)S(1)}, bf16[256,1024]{1,0:T(8,128)(2,1)S(1)}, bf16[256,1024]{1,0:T(8,128)(2,1)S(1)}, bf16[256,1024]{1,0:T(8,128)(2,1)S(1)}) fusion(pred[1024]{0:T(1024)(128)(4,1)S(1)} %get-tuple-element.20, pred[1024]{0:T(1024)(128)(4,1)S(1)} %get-tuple-element.23, pred[1024]{0:T(1024)(128)(4,1)S(1)} %get-tuple-element.22, ...), kind=kOutput, calls=%fused_computation.60 | convolution fusion | flops 539230208 | bytes 2629632 | tf_op jit(solution)/shard_map/dot_general | solution.py:227
  30.6 4.4 %fusion.35 = bf16[512,1024]{1,0:T(8,128)(2,1)} fusion(bf16[256,1024]{1,0:T(8,128)(2,1)S(1)} %get-tuple-element.13, bf16[256,1024]{1,0:T(8,128)(2,1)S(1)} %get-tuple-element.14, bf16[256,1024]{1,0:T(8,128)(2,1)S(1)} %get-tuple-element.15, bf16[256,1024]{1,0:T(8,128)(2,1)S(1)} %get-tuple-element.12, s32[1024]{0:T(1024)S(1)} %get-tuple-element.27, ...), kind=kOutput, calls=%fused_computation.39 | convolution fusion | flops 1095761920 | bytes 3174400 | tf_op jit(solution)/shard_map/dot_general | solution.py:238
  35.0 5.8 %all-to-all-start.2 = ((bf16[32,16,1024]{2,1,0:T(8,128)(2,1)}), bf16[32,16,1024]{2,1,0:T(8,128)(2,1)S(1)}, u32[]{:S(2)}, u32[]{:S(2)}) async-start(bf16[32,16,1024]{2,1,0:T(8,128)(2,1)} %bitcast.4), calls=%async_computation.2 | async-start | bytes 2097152 | tf_op jit(solution)/shard_map/all_to_all | solution.py:239
  40.8 1.0 select_convert_fusion.2.hy_ref
  41.8 0.8 broadcast_multiply_fusion.scale_ref
  42.6 1.3 select_convert_fusion
  43.9 0.7 convert_reduce_fusion
  44.7 0.1 copy.13
  44.8 0.7 reshape.1195.off_ref
  45.5 0.1 fusion.101
  45.7 0.1 select_reduce_fusion.2
  45.8 0.2 select_reduce_fusion.1
  46.0 0.7 add.593.to_ref
  46.7 20.3 %all-to-all-done.2.vals_ref = bf16[32,16,1024]{2,1,0:T(8,128)(2,1)S(1)} async-done(((bf16[32,16,1024]{2,1,0:T(8,128)(2,1)}), bf16[32,16,1024]{2,1,0:T(8,128)(2,1)S(1)}, u32[]{:S(2)}, u32[]{:S(2)}) %all-to-all-start.2) | async-done | bytes 1048608 | tf_op jit(solution)/shard_map/all_to_all | solution.py:239
  67.0 1.0 copy-done
  68.0 71.9 %shard_map.65 = f32[4,256,2048]{2,1,0:T(8,128)} custom-call(s32[1056]{0:T(1024)} %reshape.1195.off_ref, s32[1024]{0:T(1024)} %add.593.to_ref, s32[33]{0:T(128)} %copy-done.2, bf16[32,16,1024]{2,1,0:T(8,128)(2,1)} %copy-done, s32[32,1,1024]{2,1,0:T(1,128)} %copy-done.1, bf16[256,256]{1,0:T(8,128)(2,1)} %select_convert_fusion.2.hy_ref, ...), custom_call_target="tpu_custom_call" | custom-call | tf_op jit(solution)/shard_map/pallas_call | solution.py:266
  (39 shorter events, 0.4 us)
Async XLA Ops:
  1.3 8.8 %all-to-all-start.1 = ((bf16[4,2,4,512]{3,2,1,0:T(4,128)(2,1)}), bf16[4,2,4,512]{3,2,1,0:T(4,128)(2,1)S(1)}, u32[]{:S(2)}, u32[]{:S(2)}) async-start(bf16[4,2,4,512]{3,2,1,0:T(4,128)(2,1)} %broadcast_in_dim.232), calls=%async_computation.1 | async-start | bytes 65536 | tf_op jit(solution)/shard_map/all_to_all | solution.py:209
  10.8 24.1 %all-to-all-start = ((s32[32,1,1024]{2,1,0:T(1,128)}), s32[32,1,1024]{2,1,0:T(1,128)S(1)}, u32[]{:S(2)}, u32[]{:S(2)}) async-start(s32[32,1,1024]{2,1,0:T(1,128)} %broadcast_in_dim.224), calls=%async_computation | async-start | bytes 262144 | tf_op jit(solution)/shard_map/all_to_all | solution.py:206
  35.0 32.1 %copy-start.1 = (s32[32,1,1024]{2,1,0:T(1,128)}, s32[32,1,1024]{2,1,0:T(1,128)S(1)}, u32[]{:S(2)}) copy-start(s32[32,1,1024]{2,1,0:T(1,128)S(1)} %all-to-all-done.ids_ref) | copy-start | bytes 393220
  35.0 32.0 %all-to-all-start.2 = ((bf16[32,16,1024]{2,1,0:T(8,128)(2,1)}), bf16[32,16,1024]{2,1,0:T(8,128)(2,1)S(1)}, u32[]{:S(2)}, u32[]{:S(2)}) async-start(bf16[32,16,1024]{2,1,0:T(8,128)(2,1)} %bitcast.4), calls=%async_computation.2 | async-start | bytes 2097152 | tf_op jit(solution)/shard_map/all_to_all | solution.py:239
  46.0 21.0 %copy-start.2 = (s32[33]{0:T(128)}, s32[33]{0:T(128)S(1)}, u32[]{:S(2)}) copy-start(s32[33]{0:T(128)S(1)} %broadcast_multiply_fusion.2.start_ref) | copy-start | bytes 400
  67.0 1.0 copy-start
